TPU v7x, 32 devices: a whole 2x2x4 slice. The times are simulated.
32 devices in a mesh: seq: 8 (over z, x), head: 4 (over y, core).
Axes of the slice: x: 2, y: 2, z: 4, core: 2. Of those that a mesh axis runs over, the one named last changes fastest.
Arguments:
- scaled_input: bfloat16 [8192, 8192], P('seq', 'head'), may hold values from -0.059814453 to 0.059814453
- out_grad: bfloat16 [8192, 8192], P('seq', 'head'), may hold values from -1.796875 to 1.796875
- write_proj: bfloat16 [8192, 128], P('seq'), may hold values from -0.5 to 0.5
- read_proj: bfloat16 [8192, 128], P('seq'), may hold values from -0.5 to 0.5
- log_decay: float32 [128, 8192], P('head', 'seq'), may hold values from -0.8 to 0, as said below
Outputs:
- grad_input: bfloat16 [8192, 8192], P('seq', 'head')
- grad_write: bfloat16 [8192, 128], P(('seq', 'head'))
- grad_read: bfloat16 [8192, 128], P(('seq', 'head'))
Inputs may be any that keep to these rules, and one draw needn't show every extreme that they name: `log_decay`: logarithms of the per-token decays of each head.
All inputs are finite; a program needn't handle non-finite values.
Results may differ from a plain program's by a relative error of at most 0.0045.
Values sent between devices are 32-bit elements; how exact they have to be, the bound alone decides.
A program may use at most 192 MiB of HBM per device.

v0:
```python
import functools
import jax
import jax.numpy as jnp
from jax import lax
from jax.experimental import pallas as pl
from jax.experimental.pallas import tpu as pltpu
from jax.sharding import PartitionSpec as P

TILE = 128
MID = TILE // 2 - 1
CHUNK = 8
MESH = pl.DeviceIdType.MESH
F32 = jnp.float32
BF16 = jnp.bfloat16


def dot(a, b, ca, cb):
    return lax.dot_general(a, b, (((ca,), (cb,)), ((), ())), preferred_element_type=F32)


def pieces(value, count, axis):
    parts = []
    for _ in range(count):
        part = value.astype(BF16)
        parts.append(part)
        value = value - part.astype(F32)
    return jnp.concatenate(parts, axis=axis)


def fill_expand(expand_ref, heads):
    rows, width = expand_ref.shape
    size = width // heads
    row = lax.broadcasted_iota(jnp.int32, (rows, width), 0)
    col = lax.broadcasted_iota(jnp.int32, (rows, width), 1)
    low = (row % heads) * size
    expand_ref[...] = jnp.where((col >= low) & (col < low + size), 1.0, 0.0).astype(BF16)


def decays(logs):
    row = lax.broadcasted_iota(jnp.int32, (TILE, TILE), 0)
    col = lax.broadcasted_iota(jnp.int32, (TILE, TILE), 1)
    rel = jnp.where(col <= row, 1.0, 0.0) - jnp.where(col <= MID, 1.0, 0.0)
    row8 = lax.broadcasted_iota(jnp.int32, (8, TILE), 0)
    col8 = lax.broadcasted_iota(jnp.int32, (8, TILE), 1)
    first = (col8 <= MID) & (row8 != 1)
    last = (col8 > MID) & (row8 != 0)
    ends = jnp.where(first | last, 1.0, 0.0)
    parts = pieces(logs, 3, 1)
    rel = rel.astype(BF16)
    ends = ends.astype(BF16)
    rel = dot(jnp.concatenate([rel] * 3, 1), parts, 1, 1)
    ends = dot(jnp.concatenate([ends] * 3, 1), parts, 1, 1)
    return rel, ends


def spread(value, expand_ref):
    return dot(pieces(value, 2, 1), expand_ref[...], 1, 0)


def summary_kernel(heads, x_ref, g_ref, w_ref, r_ref, ld_ref, state_ref, decay_ref, expand_ref):
    k = pl.program_id(0)

    @pl.when(k == 0)
    def _():
        fill_expand(expand_ref, heads)
        state_ref[...] = jnp.zeros_like(state_ref)
        decay_ref[...] = jnp.ones_like(decay_ref)

    rel, ends = decays(ld_ref[...])
    ends = spread(jnp.exp(ends), expand_ref)
    from_start, to_end, whole = ends[0:1], ends[1:2], ends[2:3]
    xs = (x_ref[...].astype(F32) * spread(jnp.exp(-rel), expand_ref)).astype(BF16)
    gs = (g_ref[...].astype(F32) * spread(jnp.exp(rel), expand_ref)).astype(BF16)
    before = decay_ref[0:1]
    state_ref[0] = whole * state_ref[0] + to_end * dot(w_ref[...], xs, 0, 0)
    state_ref[1] += (before * from_start) * dot(r_ref[...], gs, 0, 0)
    decay_ref[...] = decay_ref[...] * whole


def chain_kernel(state_ref, decay_ref, out_ref, got, prior, passed, theirs, dec,
                 sa, ra, sb, rb, sc, rc, sd, rd):
    me = lax.axis_index("seq")
    count = lax.axis_size("seq")
    odd = lax.rem(me, 2)
    partner = me + 1 - 2 * odd
    step = 4 * odd - 2
    nxt, prv = me + step, me - step
    has_next = (nxt >= 0) & (nxt < count)
    has_prev = (prv >= 0) & (prv < count)
    fed = partner + step
    partner_prev = (fed >= 0) & (fed < count)
    mine, other = 1 - odd, odd
    barrier = pltpu.get_barrier_semaphore()
    pl.semaphore_signal(barrier, 1, device_id={"seq": partner}, device_id_type=MESH)

    @pl.when(has_next)
    def _():
        pl.semaphore_signal(barrier, 1, device_id={"seq": nxt}, device_id_type=MESH)

    @pl.when(has_prev)
    def _():
        pl.semaphore_signal(barrier, 1, device_id={"seq": prv}, device_id_type=MESH)

    peers = 1 + has_next.astype(jnp.int32) + has_prev.astype(jnp.int32)
    pl.semaphore_wait(barrier, peers)
    chunks = state_ref.shape[1] // CHUNK

    def rows(c):
        return pl.ds(c * CHUNK, CHUNK)

    def swap(c):
        return pltpu.make_async_remote_copy(
            state_ref.at[other, rows(c)], got.at[rows(c)], sa.at[c], ra.at[c],
            device_id={"seq": partner}, device_id_type=MESH)

    def forward(c):
        return pltpu.make_async_remote_copy(
            passed.at[rows(c)], prior.at[rows(c)], sb.at[c], rb.at[c],
            device_id={"seq": nxt}, device_id_type=MESH)

    def hand(c):
        return pltpu.make_async_remote_copy(
            prior.at[rows(c)], theirs.at[rows(c)], sc.at[c], rc.at[c],
            device_id={"seq": partner}, device_id_type=MESH)

    ratio = pltpu.make_async_remote_copy(
        decay_ref, dec, sd, rd, device_id={"seq": partner}, device_id_type=MESH)
    ratio.start()
    for c in range(chunks):
        swap(c).start()
    ratio.wait_recv()
    own = decay_ref[0:1]
    partners = dec[0:1]
    pair = own * partners
    for c in range(chunks):
        swap(c).wait_recv()
        summed = own * got[rows(c)] + state_ref[mine, rows(c)]

        @pl.when(has_prev)
        def _():
            forward(c).wait_recv()
            hand(c).start()
            passed[rows(c)] = pair * prior[rows(c)] + summed
            out_ref[0, rows(c)] = partners * prior[rows(c)] + got[rows(c)]

        @pl.when(jnp.logical_not(has_prev))
        def _():
            passed[rows(c)] = summed
            out_ref[0, rows(c)] = got[rows(c)]

        @pl.when(has_next)
        def _():
            forward(c).start()

    for c in range(chunks):

        @pl.when(partner_prev)
        def _():
            hand(c).wait_recv()
            out_ref[1, rows(c)] = theirs[rows(c)]

        @pl.when(jnp.logical_not(partner_prev))
        def _():
            out_ref[1, rows(c)] = jnp.zeros_like(theirs[rows(c)])

    ratio.wait_send()
    for c in range(chunks):
        swap(c).wait_send()

        @pl.when(has_prev)
        def _():
            hand(c).wait_send()

        @pl.when(has_next)
        def _():
            forward(c).wait_send()


def main_kernel(heads, tiles, x_ref, g_ref, w_ref, r_ref, ld_ref, in_ref, gi_ref, gw_ref, gr_ref,
                expand_ref, xs_ref, gs_ref, carry_ref):
    i = pl.program_id(0)
    odd = lax.rem(lax.axis_index("seq"), 2)

    @pl.when(i == 0)
    def _():
        fill_expand(expand_ref, heads)
        carry_ref[...] = in_ref[1 - odd]

    @pl.when(i == tiles)
    def _():
        carry_ref[...] = in_ref[odd]

    k = jnp.where(i < tiles, i, 2 * tiles - 1 - i)
    span = pl.ds(pl.multiple_of(k * TILE, TILE), TILE)
    rel, ends = decays(ld_ref[:, span])
    ends = spread(jnp.exp(ends), expand_ref)
    from_start, to_end, whole = ends[0:1], ends[1:2], ends[2:3]
    writes, reads = w_ref[span], r_ref[span]
    row = lax.broadcasted_iota(jnp.int32, (TILE, TILE), 0)
    col = lax.broadcasted_iota(jnp.int32, (TILE, TILE), 1)
    upper = col >= row

    @pl.when(i < tiles)
    def _():
        xs = (x_ref[...].astype(F32) * spread(jnp.exp(-rel), expand_ref)).astype(BF16)
        gs = (g_ref[...].astype(F32) * spread(jnp.exp(rel), expand_ref)).astype(BF16)
        xs_ref[span] = xs
        gs_ref[span] = gs
        weights = jnp.where(upper, dot(xs, gs, 1, 1), 0.0)
        high = weights.astype(BF16)
        entering = (from_start * carry_ref[...]).astype(BF16)
        gw_ref[span] = dot(high, reads, 1, 0)
        gr_ref[span] = dot(high, writes, 0, 0) + dot(gs, entering, 1, 1)
        carry_ref[...] = whole * carry_ref[...] + to_end * dot(writes, xs, 0, 0)

    @pl.when(i >= tiles)
    def _():
        xs = xs_ref[span]
        gs = gs_ref[span]
        leaving = (to_end * carry_ref[...]).astype(BF16)
        pairs = jnp.where(upper, dot(writes, reads, 1, 1), 0.0).astype(BF16)
        left = jnp.concatenate([pairs, writes], 1)
        right = jnp.concatenate([gs, leaving], 0)
        gi_ref[...] = (spread(jnp.exp(-rel), expand_ref) * dot(left, right, 1, 0)).astype(BF16)
        gw_ref[span] += dot(xs, leaving, 1, 1)
        carry_ref[...] = whole * carry_ref[...] + from_start * dot(reads, gs, 0, 0)


def scatter_kernel(gw_ref, gr_ref, ow_ref, or_ref, near, half, far, sa, ra, sb, rb):
    me = lax.axis_index("head")
    count = lax.axis_size("head")
    chips = count // 2
    core = lax.rem(me, 2)
    chip = me // 2
    mate = me + 1 - 2 * core
    size = ow_ref.shape[0]
    barrier = pltpu.get_barrier_semaphore()
    pl.semaphore_signal(barrier, 1, device_id={"head": mate}, device_id_type=MESH)
    for d in range(1, chips):
        there = 2 * lax.rem(chip + d, chips) + core
        pl.semaphore_signal(barrier, 1, device_id={"head": there}, device_id_type=MESH)
    pl.semaphore_wait(barrier, chips)

    def block(h):
        return pl.ds(pl.multiple_of(h * size, size), size)

    def swap(which, d):
        at = 2 * lax.rem(chip + d, chips) + 1 - core
        ref = (gw_ref, gr_ref)[which]
        return pltpu.make_async_remote_copy(
            ref.at[block(at)], near.at[which, d], sa.at[which, d], ra.at[which, d],
            device_id={"head": mate}, device_id_type=MESH)

    def cross(d):
        there = 2 * lax.rem(chip + d, chips) + core
        return pltpu.make_async_remote_copy(
            half.at[:, d], far.at[:, d], sb.at[d], rb.at[d],
            device_id={"head": there}, device_id_type=MESH)

    order = [d for d in range(1, chips)] + [0]
    for d in order:
        for which in range(2):
            swap(which, d).start()
    for d in order:
        at = 2 * lax.rem(chip + d, chips) + core
        for which, ref in enumerate((gw_ref, gr_ref)):
            swap(which, d).wait_recv()
            half[which, d] = near[which, d] + ref[block(at)]
        if d:
            cross(d).start()
    total = [half[0, 0], half[1, 0]]
    for d in range(1, chips):
        cross(d).wait_recv()
        total = [total[0] + far[0, d], total[1] + far[1, d]]
    ow_ref[...] = total[0].astype(BF16)
    or_ref[...] = total[1].astype(BF16)
    for d in order:
        for which in range(2):
            swap(which, d).wait_send()
        if d:
            cross(d).wait_send()


def body(x, g, w, r, ld, head_count):
    tokens, width = x.shape
    heads = ld.shape[0]
    state = w.shape[1]
    tiles = tokens // TILE
    limit = 60 * 1024 * 1024
    shape = jax.ShapeDtypeStruct
    vmem = pl.BlockSpec(memory_space=pltpu.VMEM)
    tile_rows = pl.BlockSpec((TILE, width), lambda k: (k, 0))
    tile_proj = pl.BlockSpec((TILE, state), lambda k: (k, 0))
    states, decay = pl.pallas_call(
        functools.partial(summary_kernel, heads),
        grid=(tiles,),
        in_specs=[tile_rows, tile_rows, tile_proj, tile_proj,
                  pl.BlockSpec((heads, TILE), lambda k: (0, k))],
        out_specs=[pl.BlockSpec((2, state, width), lambda k: (0, 0, 0)),
                   pl.BlockSpec((8, width), lambda k: (0, 0))],
        out_shape=[shape((2, state, width), F32), shape((8, width), F32)],
        scratch_shapes=[pltpu.VMEM((2 * heads, width), BF16)],
        compiler_params=pltpu.CompilerParams(vmem_limit_bytes=limit),
        name="summary",
    )(x, g, w, r, ld)
    chunks = state // CHUNK
    sem = pltpu.SemaphoreType.DMA
    buffer = pltpu.VMEM((state, width), F32)
    arriving = pl.pallas_call(
        chain_kernel,
        in_specs=[vmem, vmem],
        out_specs=vmem,
        out_shape=shape((2, state, width), F32),
        scratch_shapes=[buffer, buffer, buffer, buffer, pltpu.VMEM((8, width), F32)]
        + [sem((chunks,))] * 6 + [sem, sem],
        compiler_params=pltpu.CompilerParams(
            collective_id=0, has_side_effects=True, vmem_limit_bytes=limit),
        name="chain",
    )(states, decay)

    def early(i):
        return (jnp.minimum(i, tiles - 1), 0)

    def late(i):
        return (jnp.minimum(2 * tiles - 1 - i, tiles - 1), 0)

    whole2 = lambda i: (0, 0)
    grad_input, part_write, part_read = pl.pallas_call(
        functools.partial(main_kernel, heads, tiles),
        grid=(2 * tiles,),
        in_specs=[pl.BlockSpec((TILE, width), early), pl.BlockSpec((TILE, width), early),
                  pl.BlockSpec((tokens, state), whole2), pl.BlockSpec((tokens, state), whole2),
                  pl.BlockSpec((heads, tokens), whole2),
                  pl.BlockSpec((2, state, width), lambda i: (0, 0, 0))],
        out_specs=[pl.BlockSpec((TILE, width), late),
                   pl.BlockSpec((tokens, state), whole2), pl.BlockSpec((tokens, state), whole2)],
        out_shape=[shape((tokens, width), BF16), shape((tokens, state), F32),
                   shape((tokens, state), F32)],
        scratch_shapes=[pltpu.VMEM((2 * heads, width), BF16), pltpu.VMEM((tokens, width), BF16),
                        pltpu.VMEM((tokens, width), BF16), pltpu.VMEM((state, width), F32)],
        compiler_params=pltpu.CompilerParams(vmem_limit_bytes=limit),
        name="main",
    )(x, g, w, r, ld, arriving)
    size = tokens // head_count
    chips = head_count // 2
    grad_write, grad_read = pl.pallas_call(
        scatter_kernel,
        in_specs=[vmem, vmem],
        out_specs=[vmem, vmem],
        out_shape=[shape((size, state), BF16)] * 2,
        scratch_shapes=[pltpu.VMEM((2, chips, size, state), F32)] * 3
        + [sem((2, chips)), sem((2, chips)), sem((chips,)), sem((chips,))],
        compiler_params=pltpu.CompilerParams(
            collective_id=1, has_side_effects=True, vmem_limit_bytes=limit),
        name="scatter",
    )(part_write, part_read)
    return grad_input, grad_write, grad_read


def solution(mesh):
    return jax.shard_map(
        functools.partial(body, head_count=mesh.shape["head"]),
        mesh=mesh,
        in_specs=(
            P("seq", "head"),
            P("seq", "head"),
            P("seq", None),
            P("seq", None),
            P("head", "seq"),
        ),
        out_specs=(P("seq", "head"), P(("seq", "head"), None), P(("seq", "head"), None)),
        check_vma=False,
    )
```

profile of v0, /device:TPU:0, one launch (start us, length us, event | category | flops | bytes accessed | tf_op | source)
XLA Modules:
  0.0 108.0 jit_solution(8020154856546739962)
XLA Ops:
  0.6 11.4 %summary.1 = (f32[2,128,2048]{2,1,0:T(8,128)}, f32[8,2048]{1,0:T(8,128)}) custom-call(bf16[1024,2048]{1,0:T(8,128)(2,1)} %x_ref.3, bf16[1024,2048]{1,0:T(8,128)(2,1)} %g_ref.3, bf16[1024,128]{1,0:T(8,128)(2,1)} %w_ref.3, bf16[1024,128]{1,0:T(8,128)(2,1)} %r_ref.3, f32[32,1024]{1,0:T(8,128)} %ld_ref.3), custom_call_target="tpu_custom_call" | custom-call | tf_op jit(solution)/shard_map/summary/pallas_call | solution.py:294
  12.1 53.2 %chain.1.in_ref = f32[2,128,2048]{2,1,0:T(8,128)} custom-call(f32[2,128,2048]{2,1,0:T(8,128)} %get-tuple-element.10.state_ref, f32[8,2048]{1,0:T(8,128)} %get-tuple-element.11.decay_ref), custom_call_target="tpu_custom_call" | custom-call | tf_op jit(solution)/shard_map/chain/pallas_call | solution.py:309
  65.2 27.8 %main.1 = (bf16[1024,2048]{1,0:T(8,128)(2,1)}, f32[1024,128]{1,0:T(8,128)}, f32[1024,128]{1,0:T(8,128)}) custom-call(bf16[1024,2048]{1,0:T(8,128)(2,1)} %x_ref.3, bf16[1024,2048]{1,0:T(8,128)(2,1)} %g_ref.3, bf16[1024,128]{1,0:T(8,128)(2,1)} %w_ref.3, bf16[1024,128]{1,0:T(8,128)(2,1)} %r_ref.3, f32[32,1024]{1,0:T(8,128)} %ld_ref.3, f32[2,128,2048]{2,1,0:T(8,128)} %chain.1.in_ref), custom_call_target="tpu_custom_call" | custom-call | tf_op jit(solution)/shard_map/main/pallas_call | solution.py:328
  93.0 12.0 %scatter.1 = (bf16[256,128]{1,0:T(8,128)(2,1)}, bf16[256,128]{1,0:T(8,128)(2,1)}) custom-call(f32[1024,128]{1,0:T(8,128)} %get-tuple-element.13.gw_ref, f32[1024,128]{1,0:T(8,128)} %get-tuple-element.14.gr_ref), custom_call_target="tpu_custom_call" | custom-call | tf_op jit(solution)/shard_map/scatter/pallas_call | solution.py:346
  105.1 1.5 %copy.10 = bf16[256,128]{1,0:T(8,128)(2,1)} copy(bf16[256,128]{1,0:T(8,128)(2,1)} %get-tuple-element.21) | data formatting | bytes 131072
  106.5 1.5 %copy.11 = bf16[256,128]{1,0:T(8,128)(2,1)} copy(bf16[256,128]{1,0:T(8,128)(2,1)} %get-tuple-element.22) | data formatting | bytes 131072
where the time goes:
time: 109 us; the launch traced here: 108 us
  Pallas kernels  104 us (95%)
  local copies, waits for them, and re-layouts  2.95 us (3%)
    pallas_call x1, Pallas kernels, body(): pl.pallas_call(chain_kernel, in_specs=[vmem, vmem], out_specs=vmem, out_s...  53.2 us
    pallas_call x1, Pallas kernels, body(): pl.pallas_call(functools.partial(main_kernel, heads, tiles), grid=(2 * ti...  27.8 us
    pallas_call x1, Pallas kernels, body(): pl.pallas_call(scatter_kernel, in_specs=[vmem, vmem], out_specs=[vmem, vm...  12 us
    pallas_call x1, Pallas kernels, body(): pl.pallas_call(functools.partial(summary_kernel, heads), grid=(tiles,), i...  11.4 us
    unnamed x2, local copies, waits for them, and re-layouts  2.95 us

commit v1 on v0

v1 whole, which is shorter than its diff:
```python
import functools
import jax
import jax.numpy as jnp
from jax import lax
from jax.experimental import pallas as pl
from jax.experimental.pallas import tpu as pltpu
from jax.sharding import PartitionSpec as P

TILE = 128
MID = TILE // 2 - 1
LANES = 256
MESH = pl.DeviceIdType.MESH
F32 = jnp.float32
BF16 = jnp.bfloat16


def dot(a, b, ca, cb):
    return lax.dot_general(a, b, (((ca,), (cb,)), ((), ())), preferred_element_type=F32)


def pieces(value, count, axis):
    parts = []
    for _ in range(count):
        part = value.astype(BF16)
        parts.append(part)
        value = value - part.astype(F32)
    return jnp.concatenate(parts, axis=axis)


def fill_expand(expand_ref, heads):
    groups, rows, lanes = expand_ref.shape
    size = groups * lanes // heads
    row = lax.broadcasted_iota(jnp.int32, (rows, lanes), 0)
    col = lax.broadcasted_iota(jnp.int32, (rows, lanes), 1)
    for c in range(groups):
        low = (row % heads) * size - c * lanes
        expand_ref[c] = jnp.where((col >= low) & (col < low + size), 1.0, 0.0).astype(BF16)


def fill_decays(ld_ref, up_ref, down_ref, ends_ref):
    tokens = ld_ref.shape[1]
    tiles = tokens // TILE
    row = lax.broadcasted_iota(jnp.int32, (TILE, TILE), 0)
    col = lax.broadcasted_iota(jnp.int32, (TILE, TILE), 1)
    rel = jnp.where(col <= row, 1.0, 0.0) - jnp.where(col <= MID, 1.0, 0.0)
    rel = jnp.concatenate([rel.astype(BF16)] * 3, 1)
    for k in range(tiles):
        span = slice(k * TILE, (k + 1) * TILE)
        value = dot(rel, pieces(ld_ref[:, span], 3, 1), 1, 1)
        up_ref[span] = pieces(jnp.exp(-value), 2, 1)
        down_ref[span] = pieces(jnp.exp(value), 2, 1)
    logs = pieces(ld_ref[...], 3, 1)
    tile = lax.broadcasted_iota(jnp.int32, (tiles, tokens), 0)
    token = lax.broadcasted_iota(jnp.int32, (tiles, tokens), 1)
    low, mid, high = tile * TILE, tile * TILE + MID, (tile + 1) * TILE
    sets = [
        (token >= low) & (token <= mid),
        (token > mid) & (token < high),
        (token >= low) & (token < high),
        token <= mid,
        token > mid,
        token >= 0,
    ]
    for n, chosen in enumerate(sets):
        marks = jnp.where(chosen, 1.0, 0.0).astype(BF16)
        value = dot(jnp.concatenate([marks] * 3, 1), logs, 1, 1)
        ends_ref[n * tiles:(n + 1) * tiles] = pieces(jnp.exp(value), 2, 1)


def layer_kernel(heads, groups, x_ref, g_ref, w_ref, r_ref, ld_ref, gi_ref, gw_ref, gr_ref,
                 expand_ref, up_ref, down_ref, ends_ref, rows_ref, left_ref, xs_ref, gs_ref,
                 sp_ref, gp_ref, loc_ref, got, prior, passed, theirs, val_ref, raw_ref, stage,
                 sa, ra, sb, rb, sc, rc, so):
    i = pl.program_id(0)
    me = lax.axis_index("seq")
    count = lax.axis_size("seq")
    tokens, lanes = x_ref.shape
    state = w_ref.shape[1]
    tiles = tokens // TILE
    odd = lax.rem(me, 2)
    partner = me + 1 - 2 * odd
    step = 4 * odd - 2
    nxt, prv, fed = me + step, me - step, partner + step
    has_next = (nxt >= 0) & (nxt < count)
    has_prev = (prv >= 0) & (prv < count)
    partner_prev = (fed >= 0) & (fed < count)
    mine, other = 1 - odd, odd
    c = lax.rem(i, groups)
    phase = i // groups

    def span(k):
        return slice(k * TILE, (k + 1) * TILE)

    def swap(c):
        return pltpu.make_async_remote_copy(
            loc_ref.at[c, other], got.at[c], sa.at[c], ra.at[c],
            device_id={"seq": partner}, device_id_type=MESH)

    def forward(c):
        return pltpu.make_async_remote_copy(
            passed.at[c], prior.at[c], sb.at[c], rb.at[c],
            device_id={"seq": nxt}, device_id_type=MESH)

    def hand(c):
        return pltpu.make_async_remote_copy(
            prior.at[c], theirs.at[c], sc.at[c], rc.at[c],
            device_id={"seq": partner}, device_id_type=MESH)

    def put(c):
        at = pl.ds(pl.multiple_of(c * lanes, lanes), lanes)
        return pltpu.make_async_copy(stage.at[c], gi_ref.at[:, at], so.at[c])

    @pl.when(i == 0)
    def _():
        barrier = pltpu.get_barrier_semaphore()
        pl.semaphore_signal(barrier, 1, device_id={"seq": partner}, device_id_type=MESH)

        @pl.when(has_next)
        def _():
            pl.semaphore_signal(barrier, 1, device_id={"seq": nxt}, device_id_type=MESH)

        @pl.when(has_prev)
        def _():
            pl.semaphore_signal(barrier, 1, device_id={"seq": prv}, device_id_type=MESH)

        fill_expand(expand_ref, heads)
        fill_decays(ld_ref, up_ref, down_ref, ends_ref)
        peers = 1 + has_next.astype(jnp.int32) + has_prev.astype(jnp.int32)
        pl.semaphore_wait(barrier, peers)

    @pl.when(phase == 0)
    def _():
        expand = expand_ref[c]
        rows = dot(ends_ref[...], expand, 1, 0)
        rows_ref[c] = rows
        xs = (x_ref[...].astype(F32) * dot(up_ref[...], expand, 1, 0)).astype(BF16)
        gs = (g_ref[...].astype(F32) * dot(down_ref[...], expand, 1, 0)).astype(BF16)
        xs_ref[c] = xs
        gs_ref[c] = gs
        carry = jnp.zeros((state, lanes), F32)
        for k in range(tiles):
            start, end, whole = (rows[n * tiles + k:n * tiles + k + 1] for n in range(3))
            sp_ref[c, k] = start * carry
            carry = whole * carry + end * dot(w_ref[span(k)], xs[span(k)], 0, 0)
        loc_ref[c, 0, :state] = carry
        carry = jnp.zeros((state, lanes), F32)
        for k in reversed(range(tiles)):
            start, end, whole = (rows[n * tiles + k:n * tiles + k + 1] for n in range(3))
            gp_ref[c, k] = end * carry
            carry = whole * carry + start * dot(r_ref[span(k)], gs[span(k)], 0, 0)
        loc_ref[c, 1, :state] = carry
        decay = jnp.broadcast_to(rows[5 * tiles:5 * tiles + 1], (8, lanes))
        loc_ref[c, 0, state:] = decay
        loc_ref[c, 1, state:] = decay
        swap(c).start()

    @pl.when(i == groups - 1)
    def _():
        row = lax.broadcasted_iota(jnp.int32, (TILE, TILE), 0)
        col = lax.broadcasted_iota(jnp.int32, (TILE, TILE), 1)
        for k in range(tiles):
            pairs = jnp.where(col >= row, dot(w_ref[span(k)], r_ref[span(k)], 1, 1), 0.0)
            left_ref[span(k), :TILE] = pairs.astype(BF16)
            left_ref[span(k), TILE:] = w_ref[span(k)]
        gw_ref[...] = jnp.zeros_like(gw_ref)
        gr_ref[...] = jnp.zeros_like(gr_ref)
        raw_ref[...] = jnp.zeros_like(raw_ref)

    @pl.when(phase == 1)
    def _():
        swap(c).wait_recv()
        own = rows_ref[c, 5 * tiles:5 * tiles + 1]
        partners = got[c, state:state + 1]
        summed = own * got[c, :state] + loc_ref[c, mine, :state]

        @pl.when(has_prev)
        def _():
            forward(c).wait_recv()
            hand(c).start()
            passed[c] = (own * partners) * prior[c] + summed
            val_ref[...] = partners * prior[c] + got[c, :state]

        @pl.when(jnp.logical_not(has_prev))
        def _():
            passed[c] = summed
            val_ref[...] = got[c, :state]

        @pl.when(has_next)
        def _():
            forward(c).start()

        for k in range(tiles):
            raw_ref[span(k)] += dot(xs_ref[c, span(k)], gs_ref[c, span(k)], 1, 1)

    @pl.when(phase == 2)
    def _():
        @pl.when(partner_prev)
        def _():
            hand(c).wait_recv()
            val_ref[...] = theirs[c]

        @pl.when(jnp.logical_not(partner_prev))
        def _():
            val_ref[...] = jnp.zeros_like(val_ref)

    @pl.when(phase == 2 - odd)
    def _():
        value = val_ref[...]
        for k in range(tiles):
            scale = rows_ref[c, 3 * tiles + k:3 * tiles + k + 1]
            entering = (sp_ref[c, k] + scale * value).astype(BF16)
            gr_ref[span(k)] += dot(gs_ref[c, span(k)], entering, 1, 1)

    @pl.when(phase == 1 + odd)
    def _():
        value = val_ref[...]
        expand = expand_ref[c]
        for k in range(tiles):
            scale = rows_ref[c, 4 * tiles + k:4 * tiles + k + 1]
            leaving = (gp_ref[c, k] + scale * value).astype(BF16)
            right = jnp.concatenate([gs_ref[c, span(k)], leaving], 0)
            up = dot(up_ref[span(k)], expand, 1, 0)
            stage[c, span(k)] = (up * dot(left_ref[span(k)], right, 1, 0)).astype(BF16)
            gw_ref[span(k)] += dot(xs_ref[c, span(k)], leaving, 1, 1)
        put(c).start()

    @pl.when(i == 2 * groups)
    def _():
        row = lax.broadcasted_iota(jnp.int32, (TILE, TILE), 0)
        col = lax.broadcasted_iota(jnp.int32, (TILE, TILE), 1)
        for k in range(tiles):
            weights = jnp.where(col >= row, raw_ref[span(k)], 0.0).astype(BF16)
            gw_ref[span(k)] += dot(weights, r_ref[span(k)], 1, 0)
            gr_ref[span(k)] += dot(weights, w_ref[span(k)], 0, 0)

    @pl.when(i == 3 * groups - 1)
    def _():
        for n in range(groups):
            put(n).wait()
            swap(n).wait_send()

            @pl.when(has_prev)
            def _():
                hand(n).wait_send()

            @pl.when(has_next)
            def _():
                forward(n).wait_send()


def scatter_kernel(gw_ref, gr_ref, ow_ref, or_ref, near, half, far, sa, ra, sb, rb):
    me = lax.axis_index("head")
    count = lax.axis_size("head")
    chips = count // 2
    core = lax.rem(me, 2)
    chip = me // 2
    mate = me + 1 - 2 * core
    size = ow_ref.shape[0]
    barrier = pltpu.get_barrier_semaphore()
    pl.semaphore_signal(barrier, 1, device_id={"head": mate}, device_id_type=MESH)
    for d in range(1, chips):
        there = 2 * lax.rem(chip + d, chips) + core
        pl.semaphore_signal(barrier, 1, device_id={"head": there}, device_id_type=MESH)
    pl.semaphore_wait(barrier, chips)

    def block(h):
        return pl.ds(pl.multiple_of(h * size, size), size)

    def swap(which, d):
        at = 2 * lax.rem(chip + d, chips) + 1 - core
        ref = (gw_ref, gr_ref)[which]
        return pltpu.make_async_remote_copy(
            ref.at[block(at)], near.at[which, d], sa.at[which, d], ra.at[which, d],
            device_id={"head": mate}, device_id_type=MESH)

    def cross(d):
        there = 2 * lax.rem(chip + d, chips) + core
        return pltpu.make_async_remote_copy(
            half.at[:, d], far.at[:, d], sb.at[d], rb.at[d],
            device_id={"head": there}, device_id_type=MESH)

    order = [d for d in range(1, chips)] + [0]
    for d in order:
        for which in range(2):
            swap(which, d).start()
    for d in order:
        at = 2 * lax.rem(chip + d, chips) + core
        for which, ref in enumerate((gw_ref, gr_ref)):
            swap(which, d).wait_recv()
            half[which, d] = near[which, d] + ref[block(at)]
        if d:
            cross(d).start()
    total = [half[0, 0], half[1, 0]]
    for d in range(1, chips):
        cross(d).wait_recv()
        total = [total[0] + far[0, d], total[1] + far[1, d]]
    ow_ref[...] = total[0].astype(BF16)
    or_ref[...] = total[1].astype(BF16)
    for d in order:
        for which in range(2):
            swap(which, d).wait_send()
        if d:
            cross(d).wait_send()


def body(x, g, w, r, ld, head_count):
    tokens, width = x.shape
    heads = ld.shape[0]
    state = w.shape[1]
    tiles = tokens // TILE
    limit = 60 * 1024 * 1024
    shape = jax.ShapeDtypeStruct
    vmem = pl.BlockSpec(memory_space=pltpu.VMEM)
    sem = pltpu.SemaphoreType.DMA
    lanes = min(LANES, width)
    groups = width // lanes
    whole = lambda i: (0, 0)
    columns = pl.BlockSpec((tokens, lanes), lambda i: (0, jnp.minimum(i, groups - 1)))
    slabs = pltpu.VMEM((groups, state, lanes), F32)
    tall = pltpu.VMEM((groups, state + 8, lanes), F32)
    grad_input, part_write, part_read = pl.pallas_call(
        functools.partial(layer_kernel, heads, groups),
        grid=(3 * groups,),
        in_specs=[columns, columns,
                  pl.BlockSpec((tokens, state), whole), pl.BlockSpec((tokens, state), whole),
                  pl.BlockSpec((heads, tokens), whole)],
        out_specs=[pl.BlockSpec(memory_space=pl.ANY),
                   pl.BlockSpec((tokens, state), whole), pl.BlockSpec((tokens, state), whole)],
        out_shape=[shape((tokens, width), BF16), shape((tokens, state), F32),
                   shape((tokens, state), F32)],
        scratch_shapes=[
            pltpu.VMEM((groups, 2 * heads, lanes), BF16),
            pltpu.VMEM((tokens, 2 * heads), BF16),
            pltpu.VMEM((tokens, 2 * heads), BF16),
            pltpu.VMEM((6 * tiles, 2 * heads), BF16),
            pltpu.VMEM((groups, 6 * tiles, lanes), F32),
            pltpu.VMEM((tokens, TILE + state), BF16),
            pltpu.VMEM((groups, tokens, lanes), BF16),
            pltpu.VMEM((groups, tokens, lanes), BF16),
            pltpu.VMEM((groups, tiles, state, lanes), F32),
            pltpu.VMEM((groups, tiles, state, lanes), F32),
            pltpu.VMEM((groups, 2, state + 8, lanes), F32),
            tall, slabs, slabs, slabs,
            pltpu.VMEM((state, lanes), F32),
            pltpu.VMEM((tokens, TILE), F32),
            pltpu.VMEM((groups, tokens, lanes), BF16),
        ] + [sem((groups,))] * 7,
        compiler_params=pltpu.CompilerParams(
            collective_id=0, has_side_effects=True, vmem_limit_bytes=limit),
        name="layer",
    )(x, g, w, r, ld)
    size = tokens // head_count
    chips = head_count // 2
    grad_write, grad_read = pl.pallas_call(
        scatter_kernel,
        in_specs=[vmem, vmem],
        out_specs=[vmem, vmem],
        out_shape=[shape((size, state), BF16)] * 2,
        scratch_shapes=[pltpu.VMEM((2, chips, size, state), F32)] * 3
        + [sem((2, chips)), sem((2, chips)), sem((chips,)), sem((chips,))],
        compiler_params=pltpu.CompilerParams(
            collective_id=1, has_side_effects=True, vmem_limit_bytes=limit),
        name="scatter",
    )(part_write, part_read)
    return grad_input, grad_write, grad_read


def solution(mesh):
    return jax.shard_map(
        functools.partial(body, head_count=mesh.shape["head"]),
        mesh=mesh,
        in_specs=(
            P("seq", "head"),
            P("seq", "head"),
            P("seq", None),
            P("seq", None),
            P("head", "seq"),
        ),
        out_specs=(P("seq", "head"), P(("seq", "head"), None), P(("seq", "head"), None)),
        check_vma=False,
    )
```

time: 109 us -> 73.7 us (0.68)
  Pallas kernels: 104 us -> 66.6 us
  local copies, waits for them, and re-layouts: 2.95 us -> 6.09 us
    pallas_call x3 -> x1, Pallas kernels: 92.4 us -> 54.6 us  [body(): pl.pallas_call(functools.partial(layer_kernel, heads, groups), grid=(3 *...]
    unnamed x2 -> x7, local copies, waits for them, and re-layouts: 2.95 us -> 6.09 us
where the time goes in v1:
time: 73.7 us; the launch traced here: 73.4 us
  Pallas kernels  66.6 us (90%)
  local copies, waits for them, and re-layouts  6.09 us (8%)
    pallas_call x1, Pallas kernels, body(): pl.pallas_call(functools.partial(layer_kernel, heads, groups), grid=(3 *...  54.6 us
    pallas_call x1, Pallas kernels, body(): pl.pallas_call(scatter_kernel, in_specs=[vmem, vmem], out_specs=[vmem, vm...  12 us
    unnamed x7, local copies, waits for them, and re-layouts  6.09 us

profile of v1, /device:TPU:0, one launch (start us, length us, event | category | flops | bytes accessed | tf_op | source)
XLA Modules:
  0.0 73.4 jit_solution(2241850442668134554)
XLA Ops:
  0.6 54.6 %layer.1 = (bf16[1024,2048]{1,0:T(8,128)(2,1)}, f32[1024,128]{1,0:T(8,128)}, f32[1024,128]{1,0:T(8,128)}) custom-call(bf16[1024,2048]{1,0:T(8,128)(2,1)} %x_ref.1, bf16[1024,2048]{1,0:T(8,128)(2,1)} %g_ref.1, bf16[1024,128]{1,0:T(8,128)(2,1)} %w_ref.1, bf16[1024,128]{1,0:T(8,128)(2,1)} %r_ref.1, f32[32,1024]{1,0:T(8,128)} %ld_ref.1), custom_call_target="tpu_custom_call" | custom-call | tf_op jit(solution)/shard_map/layer/pallas_call | solution.py:321
  55.3 12.0 %scatter.1 = (bf16[256,128]{1,0:T(8,128)(2,1)}, bf16[256,128]{1,0:T(8,128)(2,1)}) custom-call(f32[1024,128]{1,0:T(8,128)} %get-tuple-element.9.gw_ref, f32[1024,128]{1,0:T(8,128)} %get-tuple-element.10.gr_ref), custom_call_target="tpu_custom_call" | custom-call | tf_op jit(solution)/shard_map/scatter/pallas_call | solution.py:354
  67.3 0.0 copy-start.1
  67.3 0.0 copy-start
  67.3 4.8 %copy.11 = bf16[1024,2048]{1,0:T(8,128)(2,1)} copy(bf16[1024,2048]{1,0:T(8,128)(2,1)} %get-tuple-element.16) | data formatting | bytes 8388608
  72.1 0.0 copy-done.1
  72.1 0.6 copy.12
  72.8 0.0 copy-done
  72.8 0.6 copy.13
Async XLA Ops:
  67.3 4.8 %copy-start.1 = (bf16[256,128]{1,0:T(8,128)(2,1)S(1)}, bf16[256,128]{1,0:T(8,128)(2,1)}, u32[]{:S(2)}) copy-start(bf16[256,128]{1,0:T(8,128)(2,1)} %get-tuple-element.17) | copy-start | bytes 196612
  67.3 5.5 %copy-start = (bf16[256,128]{1,0:T(8,128)(2,1)S(1)}, bf16[256,128]{1,0:T(8,128)(2,1)}, u32[]{:S(2)}) copy-start(bf16[256,128]{1,0:T(8,128)(2,1)} %get-tuple-element.18) | copy-start | bytes 196612

commit v2 on v1

--- a/solution.py
+++ b/solution.py
@@ -67,10 +67,10 @@
         ends_ref[n * tiles:(n + 1) * tiles] = pieces(jnp.exp(value), 2, 1)
 
 
-def layer_kernel(heads, groups, x_ref, g_ref, w_ref, r_ref, ld_ref, gi_ref, gw_ref, gr_ref,
+def layer_kernel(heads, groups, x_ref, g_ref, w_ref, r_ref, ld_ref, gi_ref, early_ref, late_ref,
                  expand_ref, up_ref, down_ref, ends_ref, rows_ref, left_ref, xs_ref, gs_ref,
                  sp_ref, gp_ref, loc_ref, got, prior, passed, theirs, val_ref, raw_ref, stage,
-                 sa, ra, sb, rb, sc, rc, so):
+                 acc_ref, near, half, far, sa, ra, sb, rb, sc, rc, so, sn, rn, sf, rf):
     i = pl.program_id(0)
     me = lax.axis_index("seq")
     count = lax.axis_size("seq")
@@ -85,6 +85,8 @@
     has_prev = (prv >= 0) & (prv < count)
     partner_prev = (fed >= 0) & (fed < count)
     mine, other = 1 - odd, odd
+    gw, gr = odd, 1 - odd
+    ring = Ring(acc_ref.at[0], near, half, far, sn, rn, sf, rf)
     c = lax.rem(i, groups)
     phase = i // groups
 
@@ -125,7 +127,8 @@
 
         fill_expand(expand_ref, heads)
         fill_decays(ld_ref, up_ref, down_ref, ends_ref)
-        peers = 1 + has_next.astype(jnp.int32) + has_prev.astype(jnp.int32)
+        ring.greet(barrier)
+        peers = ring.chips + 1 + has_next.astype(jnp.int32) + has_prev.astype(jnp.int32)
         pl.semaphore_wait(barrier, peers)
 
     @pl.when(phase == 0)
@@ -162,8 +165,7 @@
             pairs = jnp.where(col >= row, dot(w_ref[span(k)], r_ref[span(k)], 1, 1), 0.0)
             left_ref[span(k), :TILE] = pairs.astype(BF16)
             left_ref[span(k), TILE:] = w_ref[span(k)]
-        gw_ref[...] = jnp.zeros_like(gw_ref)
-        gr_ref[...] = jnp.zeros_like(gr_ref)
+        acc_ref[...] = jnp.zeros_like(acc_ref)
         raw_ref[...] = jnp.zeros_like(raw_ref)
 
     @pl.when(phase == 1)
@@ -209,7 +211,7 @@
         for k in range(tiles):
             scale = rows_ref[c, 3 * tiles + k:3 * tiles + k + 1]
             entering = (sp_ref[c, k] + scale * value).astype(BF16)
-            gr_ref[span(k)] += dot(gs_ref[c, span(k)], entering, 1, 1)
+            acc_ref[gr, span(k)] += dot(gs_ref[c, span(k)], entering, 1, 1)
 
     @pl.when(phase == 1 + odd)
     def _():
@@ -221,7 +223,7 @@
             right = jnp.concatenate([gs_ref[c, span(k)], leaving], 0)
             up = dot(up_ref[span(k)], expand, 1, 0)
             stage[c, span(k)] = (up * dot(left_ref[span(k)], right, 1, 0)).astype(BF16)
-            gw_ref[span(k)] += dot(xs_ref[c, span(k)], leaving, 1, 1)
+            acc_ref[gw, span(k)] += dot(xs_ref[c, span(k)], leaving, 1, 1)
         put(c).start()
 
     @pl.when(i == 2 * groups)
@@ -230,11 +232,22 @@
         col = lax.broadcasted_iota(jnp.int32, (TILE, TILE), 1)
         for k in range(tiles):
             weights = jnp.where(col >= row, raw_ref[span(k)], 0.0).astype(BF16)
-            gw_ref[span(k)] += dot(weights, r_ref[span(k)], 1, 0)
-            gr_ref[span(k)] += dot(weights, w_ref[span(k)], 0, 0)
+            acc_ref[gw, span(k)] += dot(weights, r_ref[span(k)], 1, 0)
+            acc_ref[gr, span(k)] += dot(weights, w_ref[span(k)], 0, 0)
+        ring.start()
+
+    @pl.when(i == 2 * groups + 1)
+    def _():
+        ring.join()
+
+    @pl.when(i == 2 * groups + 3)
+    def _():
+        early_ref[...] = ring.total()
 
     @pl.when(i == 3 * groups - 1)
     def _():
+        late_ref[...] = acc_ref[1]
+        ring.drain()
         for n in range(groups):
             put(n).wait()
             swap(n).wait_send()
@@ -248,59 +261,88 @@
                 forward(n).wait_send()
 
 
-def scatter_kernel(gw_ref, gr_ref, ow_ref, or_ref, near, half, far, sa, ra, sb, rb):
-    me = lax.axis_index("head")
-    count = lax.axis_size("head")
-    chips = count // 2
-    core = lax.rem(me, 2)
-    chip = me // 2
-    mate = me + 1 - 2 * core
-    size = ow_ref.shape[0]
+class Ring:
+    def __init__(self, source, near, half, far, sa, ra, sb, rb):
+        self.me = lax.axis_index("head")
+        self.chips = lax.axis_size("head") // 2
+        self.core = lax.rem(self.me, 2)
+        self.chip = self.me // 2
+        self.mate = self.me + 1 - 2 * self.core
+        self.order = list(range(1, self.chips)) + [0]
+        self.size = near.shape[1]
+        self.source, self.near, self.half, self.far = source, near, half, far
+        self.sems = sa, ra, sb, rb
+
+    def peer(self, d):
+        return 2 * lax.rem(self.chip + d, self.chips) + self.core
+
+    def greet(self, barrier):
+        pl.semaphore_signal(barrier, 1, device_id={"head": self.mate}, device_id_type=MESH)
+        for d in range(1, self.chips):
+            pl.semaphore_signal(barrier, 1, device_id={"head": self.peer(d)}, device_id_type=MESH)
+
+    def block(self, h):
+        return pl.ds(pl.multiple_of(h * self.size, self.size), self.size)
+
+    def swap(self, d):
+        sa, ra, _, _ = self.sems
+        at = self.peer(d) + 1 - 2 * self.core
+        return pltpu.make_async_remote_copy(
+            self.source.at[self.block(at)], self.near.at[d], sa.at[d], ra.at[d],
+            device_id={"head": self.mate}, device_id_type=MESH)
+
+    def cross(self, d):
+        _, _, sb, rb = self.sems
+        return pltpu.make_async_remote_copy(
+            self.half.at[d], self.far.at[d], sb.at[d], rb.at[d],
+            device_id={"head": self.peer(d)}, device_id_type=MESH)
+
+    def start(self):
+        for d in self.order:
+            self.swap(d).start()
+
+    def join(self):
+        for d in self.order:
+            self.swap(d).wait_recv()
+            self.half[d] = self.near[d] + self.source[self.block(self.peer(d))]
+            if d:
+                self.cross(d).start()
+
+    def total(self):
+        total = self.half[0]
+        for d in range(1, self.chips):
+            self.cross(d).wait_recv()
+            total = total + self.far[d]
+        return total.astype(BF16)
+
+    def drain(self):
+        for d in self.order:
+            self.swap(d).wait_send()
+            if d:
+                self.cross(d).wait_send()
+
+
+def scatter_kernel(early_ref, late_ref, ow_ref, or_ref, near, half, far, sa, ra, sb, rb):
+    ring = Ring(late_ref, near, half, far, sa, ra, sb, rb)
+    odd = lax.rem(lax.axis_index("seq"), 2)
     barrier = pltpu.get_barrier_semaphore()
-    pl.semaphore_signal(barrier, 1, device_id={"head": mate}, device_id_type=MESH)
-    for d in range(1, chips):
-        there = 2 * lax.rem(chip + d, chips) + core
-        pl.semaphore_signal(barrier, 1, device_id={"head": there}, device_id_type=MESH)
-    pl.semaphore_wait(barrier, chips)
-
-    def block(h):
-        return pl.ds(pl.multiple_of(h * size, size), size)
-
-    def swap(which, d):
-        at = 2 * lax.rem(chip + d, chips) + 1 - core
-        ref = (gw_ref, gr_ref)[which]
-        return pltpu.make_async_remote_copy(
-            ref.at[block(at)], near.at[which, d], sa.at[which, d], ra.at[which, d],
-            device_id={"head": mate}, device_id_type=MESH)
-
-    def cross(d):
-        there = 2 * lax.rem(chip + d, chips) + core
-        return pltpu.make_async_remote_copy(
-            half.at[:, d], far.at[:, d], sb.at[d], rb.at[d],
-            device_id={"head": there}, device_id_type=MESH)
-
-    order = [d for d in range(1, chips)] + [0]
-    for d in order:
-        for which in range(2):
-            swap(which, d).start()
-    for d in order:
-        at = 2 * lax.rem(chip + d, chips) + core
-        for which, ref in enumerate((gw_ref, gr_ref)):
-            swap(which, d).wait_recv()
-            half[which, d] = near[which, d] + ref[block(at)]
-        if d:
-            cross(d).start()
-    total = [half[0, 0], half[1, 0]]
-    for d in range(1, chips):
-        cross(d).wait_recv()
-        total = [total[0] + far[0, d], total[1] + far[1, d]]
-    ow_ref[...] = total[0].astype(BF16)
-    or_ref[...] = total[1].astype(BF16)
-    for d in order:
-        for which in range(2):
-            swap(which, d).wait_send()
-        if d:
-            cross(d).wait_send()
+    ring.greet(barrier)
+    pl.semaphore_wait(barrier, ring.chips)
+    ring.start()
+    ring.join()
+    late = ring.total()
+
+    @pl.when(odd == 1)
+    def _():
+        or_ref[...] = early_ref[...]
+        ow_ref[...] = late
+
+    @pl.when(odd == 0)
+    def _():
+        ow_ref[...] = early_ref[...]
+        or_ref[...] = late
+
+    ring.drain()
 
 
 def body(x, g, w, r, ld, head_count):
@@ -318,15 +360,18 @@
     columns = pl.BlockSpec((tokens, lanes), lambda i: (0, jnp.minimum(i, groups - 1)))
     slabs = pltpu.VMEM((groups, state, lanes), F32)
     tall = pltpu.VMEM((groups, state + 8, lanes), F32)
-    grad_input, part_write, part_read = pl.pallas_call(
+    size = tokens // head_count
+    chips = head_count // 2
+    links = [pltpu.VMEM((chips, size, state), F32)] * 3
+    grad_input, early, late = pl.pallas_call(
         functools.partial(layer_kernel, heads, groups),
         grid=(3 * groups,),
         in_specs=[columns, columns,
                   pl.BlockSpec((tokens, state), whole), pl.BlockSpec((tokens, state), whole),
                   pl.BlockSpec((heads, tokens), whole)],
         out_specs=[pl.BlockSpec(memory_space=pl.ANY),
-                   pl.BlockSpec((tokens, state), whole), pl.BlockSpec((tokens, state), whole)],
-        out_shape=[shape((tokens, width), BF16), shape((tokens, state), F32),
+                   pl.BlockSpec((size, state), whole), pl.BlockSpec((tokens, state), whole)],
+        out_shape=[shape((tokens, width), BF16), shape((size, state), BF16),
                    shape((tokens, state), F32)],
         scratch_shapes=[
             pltpu.VMEM((groups, 2 * heads, lanes), BF16),
@@ -344,24 +389,22 @@
             pltpu.VMEM((state, lanes), F32),
             pltpu.VMEM((tokens, TILE), F32),
             pltpu.VMEM((groups, tokens, lanes), BF16),
-        ] + [sem((groups,))] * 7,
+            pltpu.VMEM((2, tokens, state), F32),
+        ] + links + [sem((groups,))] * 7 + [sem((chips,))] * 4,
         compiler_params=pltpu.CompilerParams(
             collective_id=0, has_side_effects=True, vmem_limit_bytes=limit),
         name="layer",
     )(x, g, w, r, ld)
-    size = tokens // head_count
-    chips = head_count // 2
     grad_write, grad_read = pl.pallas_call(
         scatter_kernel,
         in_specs=[vmem, vmem],
         out_specs=[vmem, vmem],
         out_shape=[shape((size, state), BF16)] * 2,
-        scratch_shapes=[pltpu.VMEM((2, chips, size, state), F32)] * 3
-        + [sem((2, chips)), sem((2, chips)), sem((chips,)), sem((chips,))],
+        scratch_shapes=links + [sem((chips,))] * 4,
         compiler_params=pltpu.CompilerParams(
-            collective_id=1, has_side_effects=True, vmem_limit_bytes=limit),
+            collective_id=1, has_side_effects=True, vmem_limit_bytes=8 * 1024 * 1024),
         name="scatter",
-    )(part_write, part_read)
+    )(early, late)
     return grad_input, grad_write, grad_read
 
 

time: 73.7 us -> 75.4 us (1.023)
  local copies, waits for them, and re-layouts: 6.09 us -> 7.92 us
    pallas_call x1, Pallas kernels: 12 us -> 7.14 us  [body(): pl.pallas_call(scatter_kernel, in_specs=[vmem, vmem], out_specs=[vmem, vm...]
    pallas_call x1, Pallas kernels: 54.6 us -> 59.3 us  [body(): pl.pallas_call(functools.partial(layer_kernel, heads, groups), grid=(3 *...]
    unnamed x7, local copies, waits for them, and re-layouts: 6.09 us -> 7.92 us
where the time goes in v2:
time: 75.4 us; the launch traced here: 75 us
  Pallas kernels  66.4 us (88%)
  local copies, waits for them, and re-layouts  7.92 us (11%)
    pallas_call x1, Pallas kernels, body(): pl.pallas_call(functools.partial(layer_kernel, heads, groups), grid=(3 *...  59.3 us
    unnamed x7, local copies, waits for them, and re-layouts  7.92 us
    pallas_call x1, Pallas kernels, body(): pl.pallas_call(scatter_kernel, in_specs=[vmem, vmem], out_specs=[vmem, vm...  7.14 us

profile of v2, /device:TPU:0, one launch (start us, length us, event | category | flops | bytes accessed | tf_op | source)
XLA Modules:
  0.0 75.0 jit_solution(8770521222854577759)
XLA Ops:
  0.6 59.3 %layer.1 = (bf16[1024,2048]{1,0:T(8,128)(2,1)}, bf16[256,128]{1,0:T(8,128)(2,1)}, f32[1024,128]{1,0:T(8,128)}) custom-call(bf16[1024,2048]{1,0:T(8,128)(2,1)} %x_ref.1, bf16[1024,2048]{1,0:T(8,128)(2,1)} %g_ref.1, bf16[1024,128]{1,0:T(8,128)(2,1)} %w_ref.1, bf16[1024,128]{1,0:T(8,128)(2,1)} %r_ref.1, f32[32,1024]{1,0:T(8,128)} %ld_ref.1), custom_call_target="tpu_custom_call" | custom-call | tf_op jit(solution)/shard_map/layer/pallas_call | solution.py:366
  59.9 0.0 copy-start
  59.9 1.0 %copy-done = f32[1024,128]{1,0:T(8,128)S(1)} copy-done((f32[1024,128]{1,0:T(8,128)S(1)}, f32[1024,128]{1,0:T(8,128)}, u32[]{:S(2)}) %copy-start) | copy-done | bytes 524312
  60.9 0.0 copy-start.1
  60.9 0.8 %copy-done.1 = bf16[256,128]{1,0:T(8,128)(2,1)S(1)} copy-done((bf16[256,128]{1,0:T(8,128)(2,1)S(1)}, bf16[256,128]{1,0:T(8,128)(2,1)}, u32[]{:S(2)}) %copy-start.1) | copy-done | bytes 65560
  61.8 7.1 %scatter.1 = (bf16[256,128]{1,0:T(8,128)(2,1)S(1)}, bf16[256,128]{1,0:T(8,128)(2,1)S(1)}) custom-call(bf16[256,128]{1,0:T(8,128)(2,1)S(1)} %copy-done.1, f32[1024,128]{1,0:T(8,128)S(1)} %copy-done), custom_call_target="tpu_custom_call" | custom-call | tf_op jit(solution)/shard_map/scatter/pallas_call | solution.py:398
  68.9 4.8 %copy.11 = bf16[1024,2048]{1,0:T(8,128)(2,1)} copy(bf16[1024,2048]{1,0:T(8,128)(2,1)} %get-tuple-element.16) | data formatting | bytes 8388608
  73.7 0.6 copy.12
  74.3 0.6 copy.13
Async XLA Ops:
  59.9 1.0 %copy-start = (f32[1024,128]{1,0:T(8,128)S(1)}, f32[1024,128]{1,0:T(8,128)}, u32[]{:S(2)}) copy-start(f32[1024,128]{1,0:T(8,128)} %get-tuple-element.10.late_ref) | copy-start | bytes 1572868
  60.9 0.8 %copy-start.1 = (bf16[256,128]{1,0:T(8,128)(2,1)S(1)}, bf16[256,128]{1,0:T(8,128)(2,1)}, u32[]{:S(2)}) copy-start(bf16[256,128]{1,0:T(8,128)(2,1)} %get-tuple-element.9.early_ref) | copy-start | bytes 196612

commit v3 on v2

--- a/solution.py
+++ b/solution.py
@@ -37,7 +37,7 @@
         expand_ref[c] = jnp.where((col >= low) & (col < low + size), 1.0, 0.0).astype(BF16)
 
 
-def fill_decays(ld_ref, up_ref, down_ref, ends_ref):
+def fill_decays(ld_ref, up_ref, down_ref, ends_ref, dec_ref):
     tokens = ld_ref.shape[1]
     tiles = tokens // TILE
     row = lax.broadcasted_iota(jnp.int32, (TILE, TILE), 0)
@@ -65,12 +65,14 @@
         marks = jnp.where(chosen, 1.0, 0.0).astype(BF16)
         value = dot(jnp.concatenate([marks] * 3, 1), logs, 1, 1)
         ends_ref[n * tiles:(n + 1) * tiles] = pieces(jnp.exp(value), 2, 1)
-
-
-def layer_kernel(heads, groups, x_ref, g_ref, w_ref, r_ref, ld_ref, gi_ref, early_ref, late_ref,
+    dec_ref[...] = jnp.broadcast_to(jnp.exp(value)[:1], dec_ref.shape)
+
+
+def layer_kernel(heads, groups, x_ref, g_ref, w_ref, r_ref, ld_ref, gi_ref, ow_ref, or_ref,
                  expand_ref, up_ref, down_ref, ends_ref, rows_ref, left_ref, xs_ref, gs_ref,
-                 sp_ref, gp_ref, loc_ref, got, prior, passed, theirs, val_ref, raw_ref, stage,
-                 acc_ref, near, half, far, sa, ra, sb, rb, sc, rc, so, sn, rn, sf, rf):
+                 sp_ref, gp_ref, loc_ref, got, prior, passed, theirs, val_ref, raw_ref, dec_ref, gotdec,
+                 acc_ref, near, half, far, near2, half2, far2, sa, ra, sb, rb, sc, rc, sd, rd,
+                 sn, rn, sf, rf, sn2, rn2, sf2, rf2):
     i = pl.program_id(0)
     me = lax.axis_index("seq")
     count = lax.axis_size("seq")
@@ -87,8 +89,12 @@
     mine, other = 1 - odd, odd
     gw, gr = odd, 1 - odd
     ring = Ring(acc_ref.at[0], near, half, far, sn, rn, sf, rf)
+    ring2 = Ring(acc_ref.at[1], near2, half2, far2, sn2, rn2, sf2, rf2)
+    ratio = pltpu.make_async_remote_copy(
+        dec_ref, gotdec, sd, rd, device_id={"seq": partner}, device_id_type=MESH)
     c = lax.rem(i, groups)
     phase = i // groups
+    cols = pl.ds(pl.multiple_of(c * lanes, lanes), lanes)
 
     def span(k):
         return slice(k * TILE, (k + 1) * TILE)
@@ -108,10 +114,6 @@
             prior.at[c], theirs.at[c], sc.at[c], rc.at[c],
             device_id={"seq": partner}, device_id_type=MESH)
 
-    def put(c):
-        at = pl.ds(pl.multiple_of(c * lanes, lanes), lanes)
-        return pltpu.make_async_copy(stage.at[c], gi_ref.at[:, at], so.at[c])
-
     @pl.when(i == 0)
     def _():
         barrier = pltpu.get_barrier_semaphore()
@@ -126,10 +128,11 @@
             pl.semaphore_signal(barrier, 1, device_id={"seq": prv}, device_id_type=MESH)
 
         fill_expand(expand_ref, heads)
-        fill_decays(ld_ref, up_ref, down_ref, ends_ref)
+        fill_decays(ld_ref, up_ref, down_ref, ends_ref, dec_ref)
         ring.greet(barrier)
         peers = ring.chips + 1 + has_next.astype(jnp.int32) + has_prev.astype(jnp.int32)
         pl.semaphore_wait(barrier, peers)
+        ratio.start()
 
     @pl.when(phase == 0)
     def _():
@@ -145,20 +148,18 @@
             start, end, whole = (rows[n * tiles + k:n * tiles + k + 1] for n in range(3))
             sp_ref[c, k] = start * carry
             carry = whole * carry + end * dot(w_ref[span(k)], xs[span(k)], 0, 0)
-        loc_ref[c, 0, :state] = carry
+        loc_ref[c, 0] = carry
         carry = jnp.zeros((state, lanes), F32)
         for k in reversed(range(tiles)):
             start, end, whole = (rows[n * tiles + k:n * tiles + k + 1] for n in range(3))
             gp_ref[c, k] = end * carry
             carry = whole * carry + start * dot(r_ref[span(k)], gs[span(k)], 0, 0)
-        loc_ref[c, 1, :state] = carry
-        decay = jnp.broadcast_to(rows[5 * tiles:5 * tiles + 1], (8, lanes))
-        loc_ref[c, 0, state:] = decay
-        loc_ref[c, 1, state:] = decay
+        loc_ref[c, 1] = carry
         swap(c).start()
 
     @pl.when(i == groups - 1)
     def _():
+        ratio.wait_recv()
         row = lax.broadcasted_iota(jnp.int32, (TILE, TILE), 0)
         col = lax.broadcasted_iota(jnp.int32, (TILE, TILE), 1)
         for k in range(tiles):
@@ -172,20 +173,20 @@
     def _():
         swap(c).wait_recv()
         own = rows_ref[c, 5 * tiles:5 * tiles + 1]
-        partners = got[c, state:state + 1]
-        summed = own * got[c, :state] + loc_ref[c, mine, :state]
+        partners = dot(pieces(gotdec[...], 2, 1), expand_ref[c], 1, 0)[0:1]
+        summed = own * got[c] + loc_ref[c, mine]
 
         @pl.when(has_prev)
         def _():
             forward(c).wait_recv()
             hand(c).start()
             passed[c] = (own * partners) * prior[c] + summed
-            val_ref[...] = partners * prior[c] + got[c, :state]
+            val_ref[...] = partners * prior[c] + got[c]
 
         @pl.when(jnp.logical_not(has_prev))
         def _():
             passed[c] = summed
-            val_ref[...] = got[c, :state]
+            val_ref[...] = got[c]
 
         @pl.when(has_next)
         def _():
@@ -222,9 +223,8 @@
             leaving = (gp_ref[c, k] + scale * value).astype(BF16)
             right = jnp.concatenate([gs_ref[c, span(k)], leaving], 0)
             up = dot(up_ref[span(k)], expand, 1, 0)
-            stage[c, span(k)] = (up * dot(left_ref[span(k)], right, 1, 0)).astype(BF16)
+            gi_ref[span(k), cols] = (up * dot(left_ref[span(k)], right, 1, 0)).astype(BF16)
             acc_ref[gw, span(k)] += dot(xs_ref[c, span(k)], leaving, 1, 1)
-        put(c).start()
 
     @pl.when(i == 2 * groups)
     def _():
@@ -242,14 +242,34 @@
 
     @pl.when(i == 2 * groups + 3)
     def _():
-        early_ref[...] = ring.total()
+        early = ring.total()
+
+        @pl.when(odd == 1)
+        def _():
+            or_ref[...] = early
+
+        @pl.when(odd == 0)
+        def _():
+            ow_ref[...] = early
 
     @pl.when(i == 3 * groups - 1)
     def _():
-        late_ref[...] = acc_ref[1]
+        ring2.start()
+        ring2.join()
+        late = ring2.total()
+
+        @pl.when(odd == 1)
+        def _():
+            ow_ref[...] = late
+
+        @pl.when(odd == 0)
+        def _():
+            or_ref[...] = late
+
         ring.drain()
+        ring2.drain()
+        ratio.wait_send()
         for n in range(groups):
-            put(n).wait()
             swap(n).wait_send()
 
             @pl.when(has_prev)
@@ -322,35 +342,12 @@
                 self.cross(d).wait_send()
 
 
-def scatter_kernel(early_ref, late_ref, ow_ref, or_ref, near, half, far, sa, ra, sb, rb):
-    ring = Ring(late_ref, near, half, far, sa, ra, sb, rb)
-    odd = lax.rem(lax.axis_index("seq"), 2)
-    barrier = pltpu.get_barrier_semaphore()
-    ring.greet(barrier)
-    pl.semaphore_wait(barrier, ring.chips)
-    ring.start()
-    ring.join()
-    late = ring.total()
-
-    @pl.when(odd == 1)
-    def _():
-        or_ref[...] = early_ref[...]
-        ow_ref[...] = late
-
-    @pl.when(odd == 0)
-    def _():
-        ow_ref[...] = early_ref[...]
-        or_ref[...] = late
-
-    ring.drain()
-
-
 def body(x, g, w, r, ld, head_count):
     tokens, width = x.shape
     heads = ld.shape[0]
     state = w.shape[1]
     tiles = tokens // TILE
-    limit = 60 * 1024 * 1024
+    limit = 48 * 1024 * 1024
     shape = jax.ShapeDtypeStruct
     vmem = pl.BlockSpec(memory_space=pltpu.VMEM)
     sem = pltpu.SemaphoreType.DMA
@@ -359,20 +356,18 @@
     whole = lambda i: (0, 0)
     columns = pl.BlockSpec((tokens, lanes), lambda i: (0, jnp.minimum(i, groups - 1)))
     slabs = pltpu.VMEM((groups, state, lanes), F32)
-    tall = pltpu.VMEM((groups, state + 8, lanes), F32)
     size = tokens // head_count
     chips = head_count // 2
     links = [pltpu.VMEM((chips, size, state), F32)] * 3
-    grad_input, early, late = pl.pallas_call(
+    grad_input, grad_write, grad_read = pl.pallas_call(
         functools.partial(layer_kernel, heads, groups),
         grid=(3 * groups,),
         in_specs=[columns, columns,
                   pl.BlockSpec((tokens, state), whole), pl.BlockSpec((tokens, state), whole),
                   pl.BlockSpec((heads, tokens), whole)],
-        out_specs=[pl.BlockSpec(memory_space=pl.ANY),
-                   pl.BlockSpec((size, state), whole), pl.BlockSpec((tokens, state), whole)],
+        out_specs=[vmem, vmem, vmem],
         out_shape=[shape((tokens, width), BF16), shape((size, state), BF16),
-                   shape((tokens, state), F32)],
+                   shape((size, state), BF16)],
         scratch_shapes=[
             pltpu.VMEM((groups, 2 * heads, lanes), BF16),
             pltpu.VMEM((tokens, 2 * heads), BF16),
@@ -384,27 +379,18 @@
             pltpu.VMEM((groups, tokens, lanes), BF16),
             pltpu.VMEM((groups, tiles, state, lanes), F32),
             pltpu.VMEM((groups, tiles, state, lanes), F32),
-            pltpu.VMEM((groups, 2, state + 8, lanes), F32),
-            tall, slabs, slabs, slabs,
+            pltpu.VMEM((groups, 2, state, lanes), F32),
+            slabs, slabs, slabs, slabs,
             pltpu.VMEM((state, lanes), F32),
             pltpu.VMEM((tokens, TILE), F32),
-            pltpu.VMEM((groups, tokens, lanes), BF16),
+            pltpu.VMEM((8, heads), F32),
+            pltpu.VMEM((8, heads), F32),
             pltpu.VMEM((2, tokens, state), F32),
-        ] + links + [sem((groups,))] * 7 + [sem((chips,))] * 4,
+        ] + links * 2 + [sem((groups,))] * 6 + [sem] * 2 + [sem((chips,))] * 8,
         compiler_params=pltpu.CompilerParams(
             collective_id=0, has_side_effects=True, vmem_limit_bytes=limit),
         name="layer",
     )(x, g, w, r, ld)
-    grad_write, grad_read = pl.pallas_call(
-        scatter_kernel,
-        in_specs=[vmem, vmem],
-        out_specs=[vmem, vmem],
-        out_shape=[shape((size, state), BF16)] * 2,
-        scratch_shapes=links + [sem((chips,))] * 4,
-        compiler_params=pltpu.CompilerParams(
-            collective_id=1, has_side_effects=True, vmem_limit_bytes=8 * 1024 * 1024),
-        name="scatter",
-    )(early, late)
     return grad_input, grad_write, grad_read
 
 

time: 75.4 us -> 72.2 us (0.958)
  local copies, waits for them, and re-layouts: 7.92 us -> 6.07 us
  Pallas kernels: 66.4 us -> 65.1 us
    pallas_call x1 -> x0, Pallas kernels: 7.14 us -> none  [body(): pl.pallas_call(scatter_kernel, in_specs=[vmem, vmem], out_specs=[vmem, vm...]
    pallas_call x1, Pallas kernels: 59.3 us -> 65.1 us  [body(): pl.pallas_call(functools.partial(layer_kernel, heads, groups), grid=(3 *...]
    unnamed x7 -> x9, local copies, waits for them, and re-layouts: 7.92 us -> 6.07 us
where the time goes in v3:
time: 72.2 us; the launch traced here: 71.8 us
  Pallas kernels  65.1 us (90%)
  local copies, waits for them, and re-layouts  6.07 us (8%)
    pallas_call x1, Pallas kernels, body(): pl.pallas_call(functools.partial(layer_kernel, heads, groups), grid=(3 *...  65.1 us
    unnamed x9, local copies, waits for them, and re-layouts  6.07 us

profile of v3, /device:TPU:0, one launch (start us, length us, event | category | flops | bytes accessed | tf_op | source)
XLA Modules:
  0.0 71.8 jit_solution(2309556551227199879)
XLA Ops:
  0.6 0.0 copy-start
  0.6 0.9 %copy-done = bf16[1024,128]{1,0:T(8,128)(2,1)S(1)} copy-done((bf16[1024,128]{1,0:T(8,128)(2,1)S(1)}, bf16[1024,128]{1,0:T(8,128)(2,1)}, u32[]{:S(2)}) %copy-start) | copy-done | bytes 262168
  1.6 0.0 copy-start.1
  1.6 0.9 %copy-done.1 = bf16[1024,128]{1,0:T(8,128)(2,1)S(1)} copy-done((bf16[1024,128]{1,0:T(8,128)(2,1)S(1)}, bf16[1024,128]{1,0:T(8,128)(2,1)}, u32[]{:S(2)}) %copy-start.1) | copy-done | bytes 262168
  2.5 0.0 copy-start.2
  2.5 0.9 %copy-done.2 = f32[32,1024]{1,0:T(8,128)S(1)} copy-done((f32[32,1024]{1,0:T(8,128)S(1)}, f32[32,1024]{1,0:T(8,128)}, u32[]{:S(2)}) %copy-start.2) | copy-done | bytes 131096
  3.4 65.1 %layer.1 = (bf16[1024,2048]{1,0:T(8,128)(2,1)S(1)}, bf16[256,128]{1,0:T(8,128)(2,1)S(1)}, bf16[256,128]{1,0:T(8,128)(2,1)S(1)}) custom-call(bf16[1024,2048]{1,0:T(8,128)(2,1)} %x_ref.1, bf16[1024,2048]{1,0:T(8,128)(2,1)} %g_ref.1, bf16[1024,128]{1,0:T(8,128)(2,1)S(1)} %copy-done, bf16[1024,128]{1,0:T(8,128)(2,1)S(1)} %copy-done.1, f32[32,1024]{1,0:T(8,128)S(1)} %copy-done.2), custom_call_target="tpu_custom_call" | custom-call | tf_op jit(solution)/shard_map/layer/pallas_call | solution.py:362
  68.5 2.0 %copy.11 = bf16[1024,2048]{1,0:T(8,128)(2,1)} copy(bf16[1024,2048]{1,0:T(8,128)(2,1)S(1)} %get-tuple-element.6) | data formatting | bytes 8388608
  70.6 0.6 copy.12
  71.2 0.6 copy.13
Async XLA Ops:
  0.6 1.0 %copy-start = (bf16[1024,128]{1,0:T(8,128)(2,1)S(1)}, bf16[1024,128]{1,0:T(8,128)(2,1)}, u32[]{:S(2)}) copy-start(bf16[1024,128]{1,0:T(8,128)(2,1)} %w_ref.1) | copy-start | bytes 786436
  1.6 0.9 %copy-start.1 = (bf16[1024,128]{1,0:T(8,128)(2,1)S(1)}, bf16[1024,128]{1,0:T(8,128)(2,1)}, u32[]{:S(2)}) copy-start(bf16[1024,128]{1,0:T(8,128)(2,1)} %r_ref.1) | copy-start | bytes 786436
  2.5 0.9 %copy-start.2 = (f32[32,1024]{1,0:T(8,128)S(1)}, f32[32,1024]{1,0:T(8,128)}, u32[]{:S(2)}) copy-start(f32[32,1024]{1,0:T(8,128)} %ld_ref.1) | copy-start | bytes 393220

commit v4 on v3

--- a/solution.py
+++ b/solution.py
@@ -127,6 +127,8 @@
         def _():
             pl.semaphore_signal(barrier, 1, device_id={"seq": prv}, device_id_type=MESH)
 
+        acc_ref[...] = jnp.zeros_like(acc_ref)
+        val_ref[...] = jnp.zeros_like(val_ref)
         fill_expand(expand_ref, heads)
         fill_decays(ld_ref, up_ref, down_ref, ends_ref, dec_ref)
         ring.greet(barrier)
@@ -166,7 +168,6 @@
             pairs = jnp.where(col >= row, dot(w_ref[span(k)], r_ref[span(k)], 1, 1), 0.0)
             left_ref[span(k), :TILE] = pairs.astype(BF16)
             left_ref[span(k), TILE:] = w_ref[span(k)]
-        acc_ref[...] = jnp.zeros_like(acc_ref)
         raw_ref[...] = jnp.zeros_like(raw_ref)
 
     @pl.when(phase == 1)
@@ -206,7 +207,7 @@
         def _():
             val_ref[...] = jnp.zeros_like(val_ref)
 
-    @pl.when(phase == 2 - odd)
+    @pl.when(phase == jnp.where(odd == 1, 1, jnp.where(partner_prev, 2, 0)))
     def _():
         value = val_ref[...]
         for k in range(tiles):
@@ -214,9 +215,10 @@
             entering = (sp_ref[c, k] + scale * value).astype(BF16)
             acc_ref[gr, span(k)] += dot(gs_ref[c, span(k)], entering, 1, 1)
 
-    @pl.when(phase == 1 + odd)
+    @pl.when(phase == jnp.where((odd == 1) & partner_prev, 2, 1))
     def _():
         value = val_ref[...]
+        value = jnp.where((odd == 1) & (phase == 1), jnp.zeros_like(value), value)
         expand = expand_ref[c]
         for k in range(tiles):
             scale = rows_ref[c, 4 * tiles + k:4 * tiles + k + 1]

time: 72.2 us -> 70 us (0.970)
  Pallas kernels: 65.1 us -> 62.9 us
    pallas_call x1, Pallas kernels: 65.1 us -> 62.9 us  [body(): pl.pallas_call(functools.partial(layer_kernel, heads, groups), grid=(3 *...]
where the time goes in v4:
time: 70 us; the launch traced here: 69.6 us
  Pallas kernels  62.9 us (90%)
  local copies, waits for them, and re-layouts  6.07 us (9%)
    pallas_call x1, Pallas kernels, body(): pl.pallas_call(functools.partial(layer_kernel, heads, groups), grid=(3 *...  62.9 us
    unnamed x9, local copies, waits for them, and re-layouts  6.07 us

profile of v4, /device:TPU:0, one launch (start us, length us, event | category | flops | bytes accessed | tf_op | source)
XLA Modules:
  0.0 69.6 jit_solution(3231328162766479911)
XLA Ops:
  0.6 0.0 copy-start
  0.6 0.9 %copy-done = bf16[1024,128]{1,0:T(8,128)(2,1)S(1)} copy-done((bf16[1024,128]{1,0:T(8,128)(2,1)S(1)}, bf16[1024,128]{1,0:T(8,128)(2,1)}, u32[]{:S(2)}) %copy-start) | copy-done | bytes 262168
  1.6 0.0 copy-start.1
  1.6 0.9 %copy-done.1 = bf16[1024,128]{1,0:T(8,128)(2,1)S(1)} copy-done((bf16[1024,128]{1,0:T(8,128)(2,1)S(1)}, bf16[1024,128]{1,0:T(8,128)(2,1)}, u32[]{:S(2)}) %copy-start.1) | copy-done | bytes 262168
  2.5 0.0 copy-start.2
  2.5 0.9 %copy-done.2 = f32[32,1024]{1,0:T(8,128)S(1)} copy-done((f32[32,1024]{1,0:T(8,128)S(1)}, f32[32,1024]{1,0:T(8,128)}, u32[]{:S(2)}) %copy-start.2) | copy-done | bytes 131096
  3.4 62.9 %layer.1 = (bf16[1024,2048]{1,0:T(8,128)(2,1)S(1)}, bf16[256,128]{1,0:T(8,128)(2,1)S(1)}, bf16[256,128]{1,0:T(8,128)(2,1)S(1)}) custom-call(bf16[1024,2048]{1,0:T(8,128)(2,1)} %x_ref.1, bf16[1024,2048]{1,0:T(8,128)(2,1)} %g_ref.1, bf16[1024,128]{1,0:T(8,128)(2,1)S(1)} %copy-done, bf16[1024,128]{1,0:T(8,128)(2,1)S(1)} %copy-done.1, f32[32,1024]{1,0:T(8,128)S(1)} %copy-done.2), custom_call_target="tpu_custom_call" | custom-call | tf_op jit(solution)/shard_map/layer/pallas_call | solution.py:364
  66.3 2.0 %copy.11 = bf16[1024,2048]{1,0:T(8,128)(2,1)} copy(bf16[1024,2048]{1,0:T(8,128)(2,1)S(1)} %get-tuple-element.6) | data formatting | bytes 8388608
  68.3 0.6 copy.12
  69.0 0.6 copy.13
Async XLA Ops:
  0.6 1.0 %copy-start = (bf16[1024,128]{1,0:T(8,128)(2,1)S(1)}, bf16[1024,128]{1,0:T(8,128)(2,1)}, u32[]{:S(2)}) copy-start(bf16[1024,128]{1,0:T(8,128)(2,1)} %w_ref.1) | copy-start | bytes 786436
  1.6 0.9 %copy-start.1 = (bf16[1024,128]{1,0:T(8,128)(2,1)S(1)}, bf16[1024,128]{1,0:T(8,128)(2,1)}, u32[]{:S(2)}) copy-start(bf16[1024,128]{1,0:T(8,128)(2,1)} %r_ref.1) | copy-start | bytes 786436
  2.5 0.9 %copy-start.2 = (f32[32,1024]{1,0:T(8,128)S(1)}, f32[32,1024]{1,0:T(8,128)}, u32[]{:S(2)}) copy-start(f32[32,1024]{1,0:T(8,128)} %ld_ref.1) | copy-start | bytes 393220
